TPU v7x, 32 devices: a whole 2x2x4 slice. The times are simulated.
32 devices in a mesh: rcv: 8 (over z, y), src: 4 (over x, core).
Axes of the slice: x: 2, y: 2, z: 4, core: 2. Of those that a mesh axis runs over, the one named last changes fastest.
Arguments:
- k_op: bfloat16 [2, 3072, 3072], P(None, 'rcv', 'src'), may hold values from -0.078125 to 0.078125
- data: bfloat16 [2, 3072, 3072], P(None, 'rcv', 'src'), may hold values from -6 to 6
- factor: bfloat16 [2, 4, 768, 128], P(None, 'src', 'rcv'), may hold values from -1.796875 to 1.796875
Outputs:
- gradient: float32 [2, 4, 768, 128], P(None, 'src', 'rcv')
All inputs are finite; a program needn't handle non-finite values.
Results may differ from a plain program's by a relative error of at most 0.0019.
Values may be sent and summed in bfloat16 or wider, within the bound.
A program may use at most 64 MiB of HBM per device.

v0:
```python
import math

import jax
import jax.numpy as jnp
from jax import lax
from jax.sharding import PartitionSpec as P


def plain_dot(left, right):
    return jnp.dot(left, right, preferred_element_type=jnp.float32)


def contract_last(left, right):
    return lax.dot_general(
        left, right, (((1,), (1,)), ((), ())), preferred_element_type=jnp.float32
    )


def contract_first(left, right):
    return lax.dot_general(
        left, right, (((0,), (0,)), ((), ())), preferred_element_type=jnp.float32
    )


def body(k_op, data, factor):
    row_count = k_op.shape[1]
    receivers = row_count * lax.axis_size("rcv")
    gathered = lax.all_gather(factor, "rcv", axis=2, tiled=True)
    factor_real = gathered[0, 0]
    factor_imaginary = gathered[1, 0]
    kernel_real = k_op[0]
    kernel_imaginary = k_op[1]
    modeled_part = jnp.stack(
        [
            plain_dot(kernel_real, factor_real) - plain_dot(kernel_imaginary, factor_imaginary),
            plain_dot(kernel_real, factor_imaginary) + plain_dot(kernel_imaginary, factor_real),
        ]
    )
    modeled = lax.psum(modeled_part, "src").astype(jnp.bfloat16)
    modeled_real = modeled[0]
    modeled_imaginary = modeled[1]
    error_real = (
        contract_last(modeled_real, factor_real)
        - contract_last(modeled_imaginary, factor_imaginary)
        - data[0].astype(jnp.float32)
    ).astype(jnp.bfloat16)
    error_imaginary = (
        contract_last(modeled_real, factor_imaginary)
        + contract_last(modeled_imaginary, factor_real)
        - data[1].astype(jnp.float32)
    ).astype(jnp.bfloat16)
    weighted_part = jnp.stack(
        [
            plain_dot(error_real, factor_real) + plain_dot(error_imaginary, factor_imaginary),
            plain_dot(error_imaginary, factor_real) - plain_dot(error_real, factor_imaginary),
        ]
    )
    mirror = jnp.stack(
        [
            contract_first(error_real, modeled_real)
            + contract_first(error_imaginary, modeled_imaginary),
            contract_first(error_imaginary, modeled_real)
            - contract_first(error_real, modeled_imaginary),
        ]
    )
    weighted = lax.psum(weighted_part, "src").astype(jnp.bfloat16)
    weighted_real = weighted[0]
    weighted_imaginary = weighted[1]
    projected = jnp.stack(
        [
            contract_first(kernel_real, weighted_real)
            + contract_first(kernel_imaginary, weighted_imaginary),
            contract_first(kernel_real, weighted_imaginary)
            - contract_first(kernel_imaginary, weighted_real),
        ]
    )
    summed = lax.psum_scatter(projected + mirror, "rcv", scatter_dimension=1, tiled=True)
    scaling = 1.0 / math.sqrt(receivers)
    return (summed * scaling)[:, None]


def solution(mesh):
    return jax.shard_map(
        body,
        mesh=mesh,
        in_specs=(P(None, "rcv", "src"), P(None, "rcv", "src"), P(None, "src", "rcv", None)),
        out_specs=P(None, "src", "rcv", None),
        check_vma=False,
    )
```

profile of v0, /device:TPU:0, one launch (start us, length us, event | category | flops | bytes accessed | tf_op | source)
XLA Modules:
  0.0 163.0 jit_solution(13344070304495948577)
XLA Ops:
  6.5 33.1 %all_gather.3 = bf16[2,1,768,128]{3,2,1,0:T(8,128)(2,1)S(1)} all-gather(bf16[2,1,96,128]{3,2,1,0:T(8,128)(2,1)} %param.5), channel_id=1, replica_groups=mesh['rcv'=8,'src'=4] {'rcv'}, dimensions={2}, use_global_device_ids=true | all-gather | bytes 442368 | tf_op jit(solution)/shard_map/all_gather | solution.py:28
  39.6 1.4 fusion.20
  41.0 0.3 fusion.22
  41.4 0.3 fusion.10
  41.7 0.3 fusion.11
  42.0 14.5 %all-reduce.6 = bf16[2,384,128]{2,1,0:T(8,128)(2,1)S(1)} all-reduce(f32[2,384,128]{2,1,0:T(8,128)S(1)} %pad_maximum_fusion), channel_id=1, replica_groups=mesh['rcv'=8,'src'=4] {'src'}, use_global_device_ids=true, to_apply=%region_0.0 | all-reduce | flops 98304 | bytes 589824 | tf_op jit(solution)/shard_map/psum | solution.py:39
  56.6 0.3 fusion.36
  56.9 0.3 fusion.35
  57.2 0.6 copy-done.1
  57.9 0.3 fusion.3
  58.2 0.3 fusion.33
  58.5 0.3 fusion.2
  58.8 0.3 fusion.34
  59.1 0.3 fusion.8
  59.5 0.3 fusion.9
  59.8 14.4 %all-reduce.7 = bf16[2,384,128]{2,1,0:T(8,128)(2,1)S(1)} all-reduce(f32[2,384,128]{2,1,0:T(8,128)S(1)} %pad_maximum_fusion.1), channel_id=1, replica_groups=mesh['rcv'=8,'src'=4] {'src'}, use_global_device_ids=true, to_apply=%region_1.0 | all-reduce | flops 98304 | bytes 589824 | tf_op jit(solution)/shard_map/psum | solution.py:66
  74.3 0.3 fusion.16
  74.6 0.3 fusion.18
  74.8 0.3 fusion.37
  75.2 0.3 fusion.38
  75.5 0.3 fusion.6
  75.8 0.3 fusion.7
  76.1 0.3 fusion.4
  76.4 0.3 fusion.5
  76.7 0.1 maximum_add_fusion
  76.8 0.0 copy-start.2
  76.8 1.2 copy.13
  78.0 0.0 all-reduce.5.cloned.1.call-update
  78.0 0.6 dynamic-slice
  79.3 75.3 %all-reduce.5.cloned.1.call-done = f32[2,768,128]{2,0,1:T(2,128)} async-done(((f32[2,768,128]{2,0,1:T(2,128)}), f32[2,768,128]{2,0,1:T(2,128)}) %all-reduce.5.cloned.1.call-update) | async-done | bytes 786448
  154.5 0.9 fusion.32
  155.5 0.6 copy.14
  (7 shorter events, 0.1 us)
Async XLA Ops:
  6.5 34.5 %copy-start = (bf16[2,384,768]{2,1,0:T(8,128)(2,1)S(1)}, bf16[2,384,768]{2,1,0:T(8,128)(2,1)}, u32[]{:S(2)}) copy-start(bf16[2,384,768]{2,1,0:T(8,128)(2,1)} %param.3) | copy-start | bytes 3538948
  6.5 148.0 %all-reduce.5.cloned.1.call-start = ((), (), s32[]{:S(2)}) async-start(), calls=%async_computation | async-start | bytes 1572864
  56.6 1.3 copy-start.1
  76.8 1.2 copy-start.2
Sparse Core Ops, SparseCore 0:
  78.1 76.3 all-reduce.4
where the time goes:
time: 163 us
  waiting for transfers between devices  75.3 us (46%)
  blocking collectives  62.1 us (38%)
  between operations  14.2 us (9%)
  matrix products  7.23 us (4%)
  local copies, waits for them, and re-layouts  3.06 us (2%)
    unnamed x2, waiting for transfers between devices  75.3 us
    all_gather x1, blocking collectives, body(): gathered = lax.all_gather(factor, 'rcv', axis=2, tiled=True)  33.1 us
    psum x1, blocking collectives, body(): modeled = lax.psum(modeled_part, 'src').astype(jnp.bfloat16)  14.5 us
    psum x1, blocking collectives, body(): weighted = lax.psum(weighted_part, 'src').astype(jnp.bfloat16)  14.4 us
    dot_general x8, matrix products, plain_dot(): return jnp.dot(left, right, preferred_element_type=jnp.float32)  3.58 us
  transfers between devices with their start and end apart: 1, of which 1 were waited for; matrix products, arithmetic and copies ran while one was open for 0% of the time, Pallas kernels for 0%

commit v1 on v0

v1 whole, which is shorter than its diff:
```python
import functools
import math

import jax
import jax.numpy as jnp
from jax import lax
from jax.experimental import pallas as pl
from jax.experimental.pallas import tpu as pltpu
from jax.sharding import PartitionSpec as P

F32 = jnp.float32
BF16 = jnp.bfloat16


def dot(left, right):
    return jnp.dot(left, right, preferred_element_type=F32)


def gram(cat):
    rank = cat.shape[1] // 2
    full = lax.dot_general(cat, cat, (((0,), (0,)), ((), ())), preferred_element_type=F32)
    real = full[:rank, :rank] + full[rank:, rank:]
    imaginary = full[rank:, :rank] - full[:rank, rank:]
    return jnp.concatenate([real, imaginary], axis=1)


def complex_right(cat):
    rank = cat.shape[1] // 2
    real, imaginary = cat[:, :rank], cat[:, rank:]
    full = jnp.concatenate([cat, jnp.concatenate([-imaginary, real], axis=1)], axis=0)
    high = full.astype(BF16)
    low = (full - high.astype(F32)).astype(BF16)
    return high, low


def regroup(values, shape):
    if shape[-2] % 16 == 0 and values.shape[-2] % 16 == 0:
        return values.reshape(shape)
    return values.astype(F32).reshape(shape).astype(BF16)


def kernel(
    nz, nx, scaling,
    k_hbm, d_hbm, q_hbm, o_ref,
    a_buf, k_vm, d_vm, xt,
    g_loc, g_rx, g_xtx, g_xrx, g_fin,
    c_tx, c_rx, z_xtx, z_xrx, v_xtx, v_xrx, zw,
    y_tx, y_rx, t_tx, t_rx,
    lsem, ssem, rsem,
):
    rcv, src = lax.axis_index("rcv"), lax.axis_index("src")
    z, y = rcv // 2, rcv % 2
    x, c = src // 2, src % 2
    ypeer = {"rcv": z * 2 + 1 - y}
    cpeer = {"src": x * 2 + 1 - c}
    zpeers = [{"rcv": lax.rem(z + d, nz) * 2 + y} for d in range(1, nz)]
    xpeers = [{"src": lax.rem(x + d, nx) * 2 + c} for d in range(1, nx)]
    everyone = [ypeer, cpeer] + zpeers + xpeers
    rows, cols = k_vm.shape[1], k_vm.shape[2]
    half = rows // 2
    rank = q_hbm.shape[3]
    own = q_hbm.shape[2]
    ghalf = rank // 2

    counter = [0]
    started = []

    def remote(source, target, peer):
        at = counter[0]
        counter[0] += 1
        copy = pltpu.make_async_remote_copy(
            src_ref=source, dst_ref=target, send_sem=ssem.at[at], recv_sem=rsem.at[at],
            device_id=peer, device_id_type=pl.DeviceIdType.MESH,
        )
        copy.start()
        started.append(copy)
        return copy

    loads = [
        pltpu.make_async_copy(q_hbm.at[0, 0], a_buf.at[z, y, :, pl.ds(0, rank)], lsem.at[0]),
        pltpu.make_async_copy(q_hbm.at[1, 0], a_buf.at[z, y, :, pl.ds(rank, rank)], lsem.at[1]),
        pltpu.make_async_copy(k_hbm, k_vm, lsem.at[2]),
        pltpu.make_async_copy(d_hbm, d_vm, lsem.at[3]),
    ]
    for load in loads:
        load.start()
    barrier = pltpu.get_barrier_semaphore()
    for peer in everyone:
        pl.semaphore_signal(barrier, inc=1, device_id=peer, device_id_type=pl.DeviceIdType.MESH)
    pl.semaphore_wait(barrier, len(everyone))
    loads[0].wait()
    loads[1].wait()

    chunk = a_buf.at[z, y]
    along = [remote(chunk, chunk, peer) for peer in zpeers]
    across = [remote(chunk, chunk, ypeer)]

    loads[2].wait()
    loads[3].wait()
    for part in range(2):
        xt[:, :, :, part * rows:(part + 1) * rows] = regroup(k_vm[part].T, (nz, 2, own, rows))
    for step in range(nz - 1):
        along[step].wait_recv()
        origin = lax.rem(z - step - 1 + nz, nz)
        chunk = a_buf.at[origin, y]
        across.append(remote(chunk, chunk, ypeer))
    for part in range(2):
        xt[:, :, :, (part + 2) * rows:(part + 3) * rows] = regroup(d_vm[part].T, (nz, 2, own, rows))
    for copy in across:
        copy.wait_recv()

    a = regroup(a_buf[...], (cols, 2 * rank))
    b = jnp.concatenate([-a[:, rank:], a[:, :rank]], axis=1)

    def products(h):
        at = pl.ds(pl.multiple_of(h * half, half), half)
        first = dot(jnp.concatenate([k_vm[0, at, :], d_vm[0, at, :]], axis=0), a)
        second = dot(jnp.concatenate([k_vm[1, at, :], d_vm[1, at, :]], axis=0), b)
        return first[:half] + second[:half], first[half:] - second[half:]

    g_loc[...] = gram(a).reshape(2, ghalf, 2 * rank)
    g_core = remote(g_loc.at[1 - c], g_rx, cpeer)
    z_other, v_other = products(1 - c)
    c_tx[0] = z_other
    c_tx[1] = v_other
    zv_core = remote(c_tx, c_rx, cpeer)
    g_core.wait_recv()
    g_pair = g_loc[c] + g_rx[...]
    g_xtx[...] = g_pair
    g_across = [remote(g_xtx, g_xrx.at[i], peer) for i, peer in enumerate(xpeers)]
    z_own, v_own = products(c)
    zv_core.wait_recv()
    z_own = z_own + c_rx[0]
    v_own = v_own + c_rx[1]
    z_xtx[...] = z_own
    z_across = [remote(z_xtx, z_xrx.at[i], peer) for i, peer in enumerate(xpeers)]
    v_xtx[...] = v_own.astype(BF16)
    v_across = [remote(v_xtx, v_xrx.at[i], peer) for i, peer in enumerate(xpeers)]
    for i, copy in enumerate(g_across):
        copy.wait_recv()
        g_pair = g_pair + g_xrx[i]
    g_fin[c] = g_pair
    g_back = remote(g_fin.at[c], g_fin.at[c], cpeer)
    g_back.wait_recv()
    g_high, g_low = complex_right(g_fin[...].reshape(rank, 2 * rank))
    for i, copy in enumerate(z_across):
        copy.wait_recv()
        z_own = z_own + z_xrx[i]
    z_round = z_own.astype(BF16)
    w_own = dot(z_round, g_high) + dot(z_round, g_low)
    for i, copy in enumerate(v_across):
        copy.wait_recv()
        v_own = v_own + v_xrx[i].astype(F32)
    w_own = jnp.concatenate(
        [w_own[:, :rank] - v_own[:, :rank], w_own[:, rank:] + v_own[:, rank:]], axis=1
    ).astype(BF16)
    zw[c] = jnp.concatenate([z_round, w_own], axis=1)
    zw_core = remote(zw.at[c], zw.at[c], cpeer)
    zw_core.wait_recv()

    full = zw[...].reshape(rows, 4 * rank)
    zr, zi, wr, wi = (full[:, i * rank:(i + 1) * rank] for i in range(4))
    h_high, h_low = complex_right(gram(full[:, :2 * rank]))
    right = jnp.concatenate(
        [
            jnp.concatenate([wr, wi], axis=1),
            jnp.concatenate([wi, -wr], axis=1),
            jnp.concatenate([-zr, zi], axis=1),
            jnp.concatenate([-zi, -zr], axis=1),
        ],
        axis=0,
    )

    def gradient(side):
        left = regroup(xt[:, side], (nz * own, 4 * rows))
        q_side = regroup(a_buf[:, side], (nz * own, 2 * rank))
        total = dot(left, right) + dot(q_side, h_high) + dot(q_side, h_low)
        return total.reshape(nz, own, 2 * rank)

    y_tx[...] = gradient(1 - y).astype(BF16)
    to_y = {}
    order = list(range(1, nz)) + [0]
    for d in order:
        at = lax.rem(z + d, nz)
        to_y[d] = remote(y_tx.at[at], y_rx.at[at], ypeer)
    t_tx[...] = gradient(y)
    to_z = []
    for d in order:
        at = lax.rem(z + d, nz)
        to_y[d].wait_recv()
        mine = t_tx[at] + y_rx[at].astype(F32)
        if d:
            t_rx[1, d - 1] = mine.astype(BF16)
            to_z.append(remote(t_rx.at[1, d - 1], t_rx.at[0, d - 1], zpeers[d - 1]))
    for i, copy in enumerate(to_z):
        copy.wait_recv()
        mine = mine + t_rx[0, i].astype(F32)
    mine = mine * scaling
    o_ref[0, 0] = mine[:, :rank]
    o_ref[1, 0] = mine[:, rank:]
    for copy in started:
        copy.wait_send()


def body(nr, ns, k_op, data, factor):
    rows, cols = k_op.shape[1:]
    own, rank = factor.shape[2:]
    nz, nx = nr // 2, ns // 2
    half = rows // 2
    count = 2 * (nz - 1) + 1 + 1 + 2 + 3 * (nx - 1) + 2 + nz + (nz - 1) + 4
    slots = max(nx - 1, 1)
    scratch = [
        pltpu.VMEM((nz, 2, own, 2 * rank), BF16),
        pltpu.VMEM((2, rows, cols), BF16),
        pltpu.VMEM((2, rows, cols), BF16),
        pltpu.VMEM((nz, 2, own, 4 * rows), BF16),
        pltpu.VMEM((2, rank // 2, 2 * rank), F32),
        pltpu.VMEM((rank // 2, 2 * rank), F32),
        pltpu.VMEM((rank // 2, 2 * rank), F32),
        pltpu.VMEM((slots, rank // 2, 2 * rank), F32),
        pltpu.VMEM((2, rank // 2, 2 * rank), F32),
        pltpu.VMEM((2, half, 2 * rank), F32),
        pltpu.VMEM((2, half, 2 * rank), F32),
        pltpu.VMEM((half, 2 * rank), F32),
        pltpu.VMEM((slots, half, 2 * rank), F32),
        pltpu.VMEM((half, 2 * rank), BF16),
        pltpu.VMEM((slots, half, 2 * rank), BF16),
        pltpu.VMEM((2, half, 4 * rank), BF16),
        pltpu.VMEM((nz, own, 2 * rank), BF16),
        pltpu.VMEM((nz, own, 2 * rank), BF16),
        pltpu.VMEM((nz, own, 2 * rank), F32),
        pltpu.VMEM((2, max(nz - 1, 1), own, 2 * rank), BF16),
        pltpu.SemaphoreType.DMA((4,)),
        pltpu.SemaphoreType.DMA((count,)),
        pltpu.SemaphoreType.DMA((count,)),
    ]
    scaling = 1.0 / math.sqrt(rows * nr)
    return pl.pallas_call(
        functools.partial(kernel, nz, nx, scaling),
        out_shape=jax.ShapeDtypeStruct((2, 1, own, rank), F32),
        in_specs=[pl.BlockSpec(memory_space=pl.ANY)] * 3,
        out_specs=pl.BlockSpec(memory_space=pltpu.VMEM),
        scratch_shapes=scratch,
        compiler_params=pltpu.CompilerParams(
            collective_id=0, has_side_effects=True, vmem_limit_bytes=56 * 1024 * 1024
        ),
        name="gradient",
    )(k_op, data, factor)


def solution(mesh):
    return jax.shard_map(
        functools.partial(body, mesh.shape["rcv"], mesh.shape["src"]),
        mesh=mesh,
        in_specs=(P(None, "rcv", "src"), P(None, "rcv", "src"), P(None, "src", "rcv", None)),
        out_specs=P(None, "src", "rcv", None),
        check_vma=False,
    )
```

time: 163 us -> 40.5 us (0.25)
  waiting for transfers between devices: 75.3 us -> 0 us
  blocking collectives: 62.1 us -> 0 us
  Pallas kernels: 0 us -> 38.8 us
  between operations: 14.2 us -> 0.01 us
  matrix products: 7.23 us -> 0 us
    unnamed x2 -> x0, waiting for transfers between devices: 75.3 us -> none
    pallas_call x0 -> x1, Pallas kernels: none -> 38.8 us  [body(): pl.pallas_call(functools.partial(kernel, nz, nx, scaling), out_shape=jax....]
    all_gather x1 -> x0, blocking collectives: 33.1 us -> none  [body(): gathered = lax.all_gather(factor, 'rcv', axis=2, tiled=True)]
    psum x2 -> x0, blocking collectives: 29 us -> none  [the longest x1 14.5 us: body(): modeled = lax.psum(modeled_part, 'src').astype(jnp.bfloat16)]
    dot_general x20 -> x0, matrix products: 7.23 us -> none  [the longest x8 3.58 us: plain_dot(): return jnp.dot(left, right, preferred_element_type=jnp.float32)]
  transfers between devices with their start and end apart: 1 -> 0, of which waited for: 1 -> 0; matrix products, arithmetic and copies ran while one was open for 0% -> 0% of each run, Pallas kernels for 0% -> 0%
where the time goes in v1:
time: 40.5 us; the launch traced here: 40.4 us
  Pallas kernels  38.8 us (96%)
  local copies, waits for them, and re-layouts  1.54 us (4%)
    pallas_call x1, Pallas kernels, body(): pl.pallas_call(functools.partial(kernel, nz, nx, scaling), out_shape=jax....  38.8 us
    unnamed x1, local copies, waits for them, and re-layouts  1.54 us

profile of v1, /device:TPU:0, one launch (start us, length us, event | category | flops | bytes accessed | tf_op | source)
XLA Modules:
  0.0 40.4 jit_solution(15277902723024191220)
XLA Ops:
  0.0 38.8 %gradient.1 = f32[2,1,96,128]{3,2,1,0:T(8,128)} custom-call(bf16[2,384,768]{2,1,0:T(8,128)(2,1)} %k_hbm.1, bf16[2,384,768]{2,1,0:T(8,128)(2,1)} %d_hbm.1, bf16[2,1,96,128]{3,2,1,0:T(8,128)(2,1)} %q_hbm.1), custom_call_target="tpu_custom_call" | custom-call | tf_op jit(solution)/shard_map/gradient/pallas_call | solution.py:238
  38.8 1.5 %copy.5 = f32[2,1,96,128]{3,2,1,0:T(8,128)} copy(f32[2,1,96,128]{3,2,1,0:T(8,128)} %gradient.1) | data formatting | bytes 196608

commit v2 on v1

v2 whole, which is shorter than its diff:
```python
import functools
import math

import jax
import jax.numpy as jnp
from jax import lax
from jax.experimental import pallas as pl
from jax.experimental.pallas import tpu as pltpu
from jax.sharding import PartitionSpec as P

F32 = jnp.float32
BF16 = jnp.bfloat16


def dot(left, right):
    return jnp.dot(left, right, preferred_element_type=F32)


def gram(cat):
    rank = cat.shape[1] // 2
    full = lax.dot_general(cat, cat, (((0,), (0,)), ((), ())), preferred_element_type=F32)
    real = full[:rank, :rank] + full[rank:, rank:]
    imaginary = full[rank:, :rank] - full[:rank, rank:]
    return jnp.concatenate([real, imaginary], axis=1)


def complex_right(cat):
    rank = cat.shape[1] // 2
    real, imaginary = cat[:, :rank], cat[:, rank:]
    full = jnp.concatenate([cat, jnp.concatenate([-imaginary, real], axis=1)], axis=0)
    high = full.astype(BF16)
    low = (full - high.astype(F32)).astype(BF16)
    return high, low


def regroup(values, shape):
    if shape[-2] % 16 == 0 and values.shape[-2] % 16 == 0:
        return values.reshape(shape)
    return values.astype(F32).reshape(shape).astype(BF16)


def kernel(
    nz, nx, scaling,
    k_hbm, d_hbm, q_hbm, o_ref,
    a_buf, k_vm, d_vm, xt,
    g_loc, g_rx, g_xtx, g_xrx, g_ytx, g_yrx, g_fin,
    c_tx, c_rx, z_xtx, z_xrx, v_xtx, v_xrx, z_all, w_all,
    y_tx, y_rx, total, t_tx, t_rx,
    lsem, ssem, rsem, zsend, zrecv,
):
    rcv, src = lax.axis_index("rcv"), lax.axis_index("src")
    z, y = rcv // 2, rcv % 2
    x, c = src // 2, src % 2
    ypeer = {"rcv": z * 2 + 1 - y}
    cpeer = {"src": x * 2 + 1 - c}
    low = z < nz // 2
    far = []
    for step in range(nz - 1):
        down, up = nz - 1 - step, step
        down = jnp.where(down <= z, down - 1, down)
        up = jnp.where(up >= z, up + 1, up)
        far.append(jnp.where(low, down, up))
    zpeers = [{"rcv": other * 2 + y} for other in far]
    xpeers = [{"src": lax.rem(x + d, nx) * 2 + c} for d in range(1, nx)]
    everyone = [ypeer, cpeer] + zpeers + xpeers
    rows, cols = k_vm.shape[1], k_vm.shape[2]
    half = rows // 2
    rank = q_hbm.shape[3]
    own = q_hbm.shape[2]
    ghalf = rank // 2

    counter = [0]
    started = []

    def remote(source, target, peer):
        at = counter[0]
        counter[0] += 1
        copy = pltpu.make_async_remote_copy(
            src_ref=source, dst_ref=target, send_sem=ssem.at[at], recv_sem=rsem.at[at],
            device_id=peer, device_id_type=pl.DeviceIdType.MESH,
        )
        copy.start()
        started.append(copy)
        return copy

    def along_z(phase, source, target, other):
        copy = pltpu.make_async_remote_copy(
            src_ref=source, dst_ref=target,
            send_sem=zsend.at[phase, other], recv_sem=zrecv.at[phase, z],
            device_id={"rcv": other * 2 + y}, device_id_type=pl.DeviceIdType.MESH,
        )
        copy.start()
        started.append(copy)

    def from_z(phase, target, other):
        pltpu.make_async_remote_copy(
            src_ref=target, dst_ref=target,
            send_sem=zsend.at[phase, other], recv_sem=zrecv.at[phase, other],
            device_id={"rcv": other * 2 + y}, device_id_type=pl.DeviceIdType.MESH,
        ).wait_recv()

    loads = [
        pltpu.make_async_copy(q_hbm.at[0, 0], a_buf.at[z, y, :, pl.ds(0, rank)], lsem.at[0]),
        pltpu.make_async_copy(q_hbm.at[1, 0], a_buf.at[z, y, :, pl.ds(rank, rank)], lsem.at[1]),
        pltpu.make_async_copy(k_hbm, k_vm, lsem.at[2]),
        pltpu.make_async_copy(d_hbm, d_vm, lsem.at[3]),
    ]
    for load in loads:
        load.start()
    barrier = pltpu.get_barrier_semaphore()
    for peer in everyone:
        pl.semaphore_signal(barrier, inc=1, device_id=peer, device_id_type=pl.DeviceIdType.MESH)
    pl.semaphore_wait(barrier, len(everyone))
    loads[0].wait()
    loads[1].wait()

    chunk = a_buf.at[z, y]
    for other in far:
        along_z(0, chunk, chunk, other)
    across = [remote(chunk, chunk, ypeer)]
    for other in far[::-1]:
        chunk = a_buf.at[other, y]
        from_z(0, chunk, other)
        across.append(remote(chunk, chunk, ypeer))

    g_loc[...] = gram(regroup(a_buf[:, y], (nz * own, 2 * rank))).reshape(2, ghalf, 2 * rank)
    g_core = remote(g_loc.at[1 - c], g_rx, cpeer)
    g_core.wait_recv()
    g_pair = g_loc[c] + g_rx[...]
    g_xtx[...] = g_pair
    g_across = [remote(g_xtx, g_xrx.at[i], peer) for i, peer in enumerate(xpeers)]

    for copy in across:
        copy.wait_recv()
    a = regroup(a_buf[...], (cols, 2 * rank))
    b = jnp.concatenate([-a[:, rank:], a[:, :rank]], axis=1)
    loads[2].wait()
    loads[3].wait()

    def product(ref, h, sign):
        at = pl.ds(pl.multiple_of(h * half, half), half)
        return dot(ref[0, at, :], a) + sign * dot(ref[1, at, :], b)

    c_tx[0] = product(k_vm, 1 - c, 1.0)
    z_core = remote(c_tx.at[0], c_rx.at[0], cpeer)
    z_own = product(k_vm, c, 1.0)
    c_tx[1] = product(d_vm, 1 - c, -1.0)
    v_core = remote(c_tx.at[1], c_rx.at[1], cpeer)
    z_core.wait_recv()
    z_own = z_own + c_rx[0]
    z_xtx[...] = z_own
    z_across = [remote(z_xtx, z_xrx.at[i], peer) for i, peer in enumerate(xpeers)]
    v_own = product(d_vm, c, -1.0)
    v_core.wait_recv()
    v_own = v_own + c_rx[1]
    v_xtx[...] = v_own.astype(BF16)
    v_across = [remote(v_xtx, v_xrx.at[i], peer) for i, peer in enumerate(xpeers)]
    for part in range(2):
        xt[:, :, :, part * rows:(part + 1) * rows] = regroup(k_vm[part].T, (nz, 2, own, rows))
        xt[:, :, :, (part + 2) * rows:(part + 3) * rows] = regroup(d_vm[part].T, (nz, 2, own, rows))
    for i, copy in enumerate(g_across):
        copy.wait_recv()
        g_pair = g_pair + g_xrx[i]
    g_ytx[...] = g_pair
    g_side = remote(g_ytx, g_yrx, ypeer)
    g_side.wait_recv()
    g_fin[c] = g_pair + g_yrx[...]
    g_back = remote(g_fin.at[c], g_fin.at[c], cpeer)
    g_back.wait_recv()
    g_high, g_low = complex_right(g_fin[...].reshape(rank, 2 * rank))
    for i, copy in enumerate(z_across):
        copy.wait_recv()
        z_own = z_own + z_xrx[i]
    z_round = z_own.astype(BF16)
    z_all[c] = z_round
    z_back = remote(z_all.at[c], z_all.at[c], cpeer)
    w_own = dot(z_round, g_high) + dot(z_round, g_low)
    z_back.wait_recv()

    z_cat = z_all[...].reshape(rows, 2 * rank)
    zr, zi = z_cat[:, :rank], z_cat[:, rank:]
    h_high, h_low = complex_right(gram(z_cat))
    z_right = jnp.concatenate(
        [jnp.concatenate([-zr, zi], axis=1), jnp.concatenate([-zi, -zr], axis=1)], axis=0
    )
    for side in range(2):
        left = regroup(xt[:, side, :, 2 * rows:], (nz * own, 2 * rows))
        q_side = regroup(a_buf[:, side], (nz * own, 2 * rank))
        total[side] = dot(left, z_right) + dot(q_side, h_high) + dot(q_side, h_low)

    for i, copy in enumerate(v_across):
        copy.wait_recv()
        v_own = v_own + v_xrx[i].astype(F32)
    w_all[c] = jnp.concatenate(
        [w_own[:, :rank] - v_own[:, :rank], w_own[:, rank:] + v_own[:, rank:]], axis=1
    ).astype(BF16)
    w_back = remote(w_all.at[c], w_all.at[c], cpeer)
    w_back.wait_recv()
    w_cat = w_all[...].reshape(rows, 2 * rank)
    wr, wi = w_cat[:, :rank], w_cat[:, rank:]
    w_right = jnp.concatenate([w_cat, jnp.concatenate([wi, -wr], axis=1)], axis=0)

    def gradient(side):
        left = regroup(xt[:, side, :, :2 * rows], (nz * own, 2 * rows))
        return (total[side] + dot(left, w_right)).reshape(nz, own, 2 * rank)

    y_tx[...] = gradient(1 - y).astype(BF16)
    to_y = [remote(y_tx.at[at], y_rx.at[at], ypeer) for at in far + [z]]
    t_tx[...] = gradient(y)
    for at, copy in zip(far, to_y):
        copy.wait_recv()
        t_rx[1, at] = (t_tx[at] + y_rx[at].astype(F32)).astype(BF16)
        along_z(1, t_rx.at[1, at], t_rx.at[0, z], at)
    to_y[-1].wait_recv()
    mine = t_tx[z] + y_rx[z].astype(F32)
    for other in far[::-1]:
        from_z(1, t_rx.at[0, other], other)
        mine = mine + t_rx[0, other].astype(F32)
    mine = mine * scaling
    o_ref[0, 0] = mine[:, :rank]
    o_ref[1, 0] = mine[:, rank:]
    for copy in started:
        copy.wait_send()


def body(nr, ns, k_op, data, factor):
    rows, cols = k_op.shape[1:]
    own, rank = factor.shape[2:]
    nz, nx = nr // 2, ns // 2
    half = rows // 2
    count = 2 * nz + 3 * (nx - 1) + 7
    slots = max(nx - 1, 1)
    scratch = [
        pltpu.VMEM((nz, 2, own, 2 * rank), BF16),
        pltpu.VMEM((2, rows, cols), BF16),
        pltpu.VMEM((2, rows, cols), BF16),
        pltpu.VMEM((nz, 2, own, 4 * rows), BF16),
        pltpu.VMEM((2, rank // 2, 2 * rank), F32),
        pltpu.VMEM((rank // 2, 2 * rank), F32),
        pltpu.VMEM((rank // 2, 2 * rank), F32),
        pltpu.VMEM((slots, rank // 2, 2 * rank), F32),
        pltpu.VMEM((rank // 2, 2 * rank), F32),
        pltpu.VMEM((rank // 2, 2 * rank), F32),
        pltpu.VMEM((2, rank // 2, 2 * rank), F32),
        pltpu.VMEM((2, half, 2 * rank), F32),
        pltpu.VMEM((2, half, 2 * rank), F32),
        pltpu.VMEM((half, 2 * rank), F32),
        pltpu.VMEM((slots, half, 2 * rank), F32),
        pltpu.VMEM((half, 2 * rank), BF16),
        pltpu.VMEM((slots, half, 2 * rank), BF16),
        pltpu.VMEM((2, half, 2 * rank), BF16),
        pltpu.VMEM((2, half, 2 * rank), BF16),
        pltpu.VMEM((nz, own, 2 * rank), BF16),
        pltpu.VMEM((nz, own, 2 * rank), BF16),
        pltpu.VMEM((2, nz * own, 2 * rank), F32),
        pltpu.VMEM((nz, own, 2 * rank), F32),
        pltpu.VMEM((2, nz, own, 2 * rank), BF16),
        pltpu.SemaphoreType.DMA((4,)),
        pltpu.SemaphoreType.DMA((count,)),
        pltpu.SemaphoreType.DMA((count,)),
        pltpu.SemaphoreType.DMA((2, nz)),
        pltpu.SemaphoreType.DMA((2, nz)),
    ]
    scaling = 1.0 / math.sqrt(rows * nr)
    return pl.pallas_call(
        functools.partial(kernel, nz, nx, scaling),
        out_shape=jax.ShapeDtypeStruct((2, 1, own, rank), F32),
        in_specs=[pl.BlockSpec(memory_space=pl.ANY)] * 3,
        out_specs=pl.BlockSpec(memory_space=pltpu.VMEM),
        scratch_shapes=scratch,
        compiler_params=pltpu.CompilerParams(
            collective_id=0, has_side_effects=True, vmem_limit_bytes=56 * 1024 * 1024
        ),
        name="gradient",
    )(k_op, data, factor)


def solution(mesh):
    return jax.shard_map(
        functools.partial(body, mesh.shape["rcv"], mesh.shape["src"]),
        mesh=mesh,
        in_specs=(P(None, "rcv", "src"), P(None, "rcv", "src"), P(None, "src", "rcv", None)),
        out_specs=P(None, "src", "rcv", None),
        check_vma=False,
    )
```

time: 40.5 us -> 37.7 us (0.931)
  Pallas kernels: 38.8 us -> 36 us
    pallas_call x1, Pallas kernels: 38.8 us -> 36 us  [body(): pl.pallas_call(functools.partial(kernel, nz, nx, scaling), out_shape=jax....]
where the time goes in v2:
time: 37.7 us; the launch traced here: 37.6 us
  Pallas kernels  36 us (95%)
  local copies, waits for them, and re-layouts  1.54 us (4%)
    pallas_call x1, Pallas kernels, body(): pl.pallas_call(functools.partial(kernel, nz, nx, scaling), out_shape=jax....  36 us
    unnamed x1, local copies, waits for them, and re-layouts  1.54 us

profile of v2, /device:TPU:0, one launch (start us, length us, event | category | flops | bytes accessed | tf_op | source)
XLA Modules:
  0.0 37.6 jit_solution(12738324471867741776)
XLA Ops:
  0.0 36.0 %gradient.1 = f32[2,1,96,128]{3,2,1,0:T(8,128)} custom-call(bf16[2,384,768]{2,1,0:T(8,128)(2,1)} %k_hbm.1, bf16[2,384,768]{2,1,0:T(8,128)(2,1)} %d_hbm.1, bf16[2,1,96,128]{3,2,1,0:T(8,128)(2,1)} %q_hbm.1), custom_call_target="tpu_custom_call" | custom-call | tf_op jit(solution)/shard_map/gradient/pallas_call | solution.py:265
  36.0 1.5 %copy.5 = f32[2,1,96,128]{3,2,1,0:T(8,128)} copy(f32[2,1,96,128]{3,2,1,0:T(8,128)} %gradient.1) | data formatting | bytes 196608

commit v3 on v2

--- a/solution.py
+++ b/solution.py
@@ -46,7 +46,7 @@
     g_loc, g_rx, g_xtx, g_xrx, g_ytx, g_yrx, g_fin,
     c_tx, c_rx, z_xtx, z_xrx, v_xtx, v_xrx, z_all, w_all,
     y_tx, y_rx, total, t_tx, t_rx,
-    lsem, ssem, rsem, zsend, zrecv,
+    lsem, ssem, rsem, zsend, zrecv, upper, lower,
 ):
     rcv, src = lax.axis_index("rcv"), lax.axis_index("src")
     z, y = rcv // 2, rcv % 2
@@ -60,9 +60,8 @@
         down = jnp.where(down <= z, down - 1, down)
         up = jnp.where(up >= z, up + 1, up)
         far.append(jnp.where(low, down, up))
-    zpeers = [{"rcv": other * 2 + y} for other in far]
     xpeers = [{"src": lax.rem(x + d, nx) * 2 + c} for d in range(1, nx)]
-    everyone = [ypeer, cpeer] + zpeers + xpeers
+    near = [ypeer, cpeer] + xpeers
     rows, cols = k_vm.shape[1], k_vm.shape[2]
     half = rows // 2
     rank = q_hbm.shape[3]
@@ -90,7 +89,6 @@
             device_id={"rcv": other * 2 + y}, device_id_type=pl.DeviceIdType.MESH,
         )
         copy.start()
-        started.append(copy)
 
     def from_z(phase, target, other):
         pltpu.make_async_remote_copy(
@@ -108,16 +106,56 @@
     for load in loads:
         load.start()
     barrier = pltpu.get_barrier_semaphore()
-    for peer in everyone:
+    for peer in near:
         pl.semaphore_signal(barrier, inc=1, device_id=peer, device_id_type=pl.DeviceIdType.MESH)
-    pl.semaphore_wait(barrier, len(everyone))
+
+    def signal_z(semaphore, other):
+        pl.semaphore_signal(
+            semaphore, inc=1, device_id={"rcv": other * 2 + y}, device_id_type=pl.DeviceIdType.MESH
+        )
+
+    @pl.when(z > 0)
+    def _():
+        signal_z(barrier, z - 1)
+
+    @pl.when(z < nz - 1)
+    def _():
+        signal_z(barrier, z + 1)
+
+    beside = jnp.where(z > 0, 1, 0) + jnp.where(z < nz - 1, 1, 0)
+    pl.semaphore_wait(barrier, len(near) + beside)
+
+    def tell(k):
+        @pl.when((z > 0) & (z + k < nz))
+        def _():
+            signal_z(upper.at[k - 1], z - 1)
+
+        @pl.when((z < nz - 1) & (z - k >= 0))
+        def _():
+            signal_z(lower.at[k - 1], z + 1)
+
+    if nz > 2:
+        tell(1)
     loads[0].wait()
     loads[1].wait()
 
     chunk = a_buf.at[z, y]
-    for other in far:
-        along_z(0, chunk, chunk, other)
     across = [remote(chunk, chunk, ypeer)]
+    for k in range(1, nz):
+        @pl.when(z + k < nz)
+        def _():
+            if k > 1:
+                pl.semaphore_wait(upper.at[k - 2], 1)
+            along_z(0, chunk, chunk, z + k)
+
+        @pl.when(z - k >= 0)
+        def _():
+            if k > 1:
+                pl.semaphore_wait(lower.at[k - 2], 1)
+            along_z(0, chunk, chunk, z - k)
+
+        if 1 < k < nz - 1:
+            tell(k)
     for other in far[::-1]:
         chunk = a_buf.at[other, y]
         from_z(0, chunk, other)
@@ -221,6 +259,13 @@
     o_ref[1, 0] = mine[:, rank:]
     for copy in started:
         copy.wait_send()
+    for other in far:
+        for phase, sent in enumerate((a_buf.at[z, y], t_rx.at[1, other])):
+            pltpu.make_async_remote_copy(
+                src_ref=sent, dst_ref=sent,
+                send_sem=zsend.at[phase, other], recv_sem=zrecv.at[phase, other],
+                device_id={"rcv": other * 2 + y}, device_id_type=pl.DeviceIdType.MESH,
+            ).wait_send()
 
 
 def body(nr, ns, k_op, data, factor):
@@ -260,6 +305,8 @@
         pltpu.SemaphoreType.DMA((count,)),
         pltpu.SemaphoreType.DMA((2, nz)),
         pltpu.SemaphoreType.DMA((2, nz)),
+        pltpu.SemaphoreType.REGULAR((nz,)),
+        pltpu.SemaphoreType.REGULAR((nz,)),
     ]
     scaling = 1.0 / math.sqrt(rows * nr)
     return pl.pallas_call(

time: 37.7 us -> 36.7 us (0.973)
  Pallas kernels: 36 us -> 35 us
    pallas_call x1, Pallas kernels: 36 us -> 35 us  [body(): pl.pallas_call(functools.partial(kernel, nz, nx, scaling), out_shape=jax....]
where the time goes in v3:
time: 36.7 us; the launch traced here: 36.5 us
  Pallas kernels  35 us (95%)
  local copies, waits for them, and re-layouts  1.54 us (4%)
    pallas_call x1, Pallas kernels, body(): pl.pallas_call(functools.partial(kernel, nz, nx, scaling), out_shape=jax....  35 us
    unnamed x1, local copies, waits for them, and re-layouts  1.54 us

profile of v3, /device:TPU:0, one launch (start us, length us, event | category | flops | bytes accessed | tf_op | source)
XLA Modules:
  0.0 36.5 jit_solution(9932702510488174652)
XLA Ops:
  0.0 35.0 %gradient.1 = f32[2,1,96,128]{3,2,1,0:T(8,128)} custom-call(bf16[2,384,768]{2,1,0:T(8,128)(2,1)} %k_hbm.1, bf16[2,384,768]{2,1,0:T(8,128)(2,1)} %d_hbm.1, bf16[2,1,96,128]{3,2,1,0:T(8,128)(2,1)} %q_hbm.1), custom_call_target="tpu_custom_call" | custom-call | tf_op jit(solution)/shard_map/gradient/pallas_call | solution.py:312
  35.0 1.5 %copy.5 = f32[2,1,96,128]{3,2,1,0:T(8,128)} copy(f32[2,1,96,128]{3,2,1,0:T(8,128)} %gradient.1) | data formatting | bytes 196608

commit v4 on v3

--- a/solution.py
+++ b/solution.py
@@ -140,26 +140,31 @@
     loads[1].wait()
 
     chunk = a_buf.at[z, y]
+    def halves(ref):
+        return [ref.at[:, pl.ds(part * rank, rank)] for part in range(2)]
+
     across = [remote(chunk, chunk, ypeer)]
     for k in range(1, nz):
         @pl.when(z + k < nz)
         def _():
             if k > 1:
                 pl.semaphore_wait(upper.at[k - 2], 1)
-            along_z(0, chunk, chunk, z + k)
+            for part, piece in enumerate(halves(chunk)):
+                along_z(part, piece, piece, z + k)
 
         @pl.when(z - k >= 0)
         def _():
             if k > 1:
                 pl.semaphore_wait(lower.at[k - 2], 1)
-            along_z(0, chunk, chunk, z - k)
+            for part, piece in enumerate(halves(chunk)):
+                along_z(part, piece, piece, z - k)
 
         if 1 < k < nz - 1:
             tell(k)
     for other in far[::-1]:
-        chunk = a_buf.at[other, y]
-        from_z(0, chunk, other)
-        across.append(remote(chunk, chunk, ypeer))
+        for part, piece in enumerate(halves(a_buf.at[other, y])):
+            from_z(part, piece, other)
+            across.append(remote(piece, piece, ypeer))
 
     g_loc[...] = gram(regroup(a_buf[:, y], (nz * own, 2 * rank))).reshape(2, ghalf, 2 * rank)
     g_core = remote(g_loc.at[1 - c], g_rx, cpeer)
@@ -182,12 +187,12 @@
     c_tx[0] = product(k_vm, 1 - c, 1.0)
     z_core = remote(c_tx.at[0], c_rx.at[0], cpeer)
     z_own = product(k_vm, c, 1.0)
-    c_tx[1] = product(d_vm, 1 - c, -1.0)
-    v_core = remote(c_tx.at[1], c_rx.at[1], cpeer)
     z_core.wait_recv()
     z_own = z_own + c_rx[0]
     z_xtx[...] = z_own
     z_across = [remote(z_xtx, z_xrx.at[i], peer) for i, peer in enumerate(xpeers)]
+    c_tx[1] = product(d_vm, 1 - c, -1.0)
+    v_core = remote(c_tx.at[1], c_rx.at[1], cpeer)
     v_own = product(d_vm, c, -1.0)
     v_core.wait_recv()
     v_own = v_own + c_rx[1]
@@ -248,11 +253,11 @@
     for at, copy in zip(far, to_y):
         copy.wait_recv()
         t_rx[1, at] = (t_tx[at] + y_rx[at].astype(F32)).astype(BF16)
-        along_z(1, t_rx.at[1, at], t_rx.at[0, z], at)
+        along_z(2, t_rx.at[1, at], t_rx.at[0, z], at)
     to_y[-1].wait_recv()
     mine = t_tx[z] + y_rx[z].astype(F32)
     for other in far[::-1]:
-        from_z(1, t_rx.at[0, other], other)
+        from_z(2, t_rx.at[0, other], other)
         mine = mine + t_rx[0, other].astype(F32)
     mine = mine * scaling
     o_ref[0, 0] = mine[:, :rank]
@@ -260,7 +265,7 @@
     for copy in started:
         copy.wait_send()
     for other in far:
-        for phase, sent in enumerate((a_buf.at[z, y], t_rx.at[1, other])):
+        for phase, sent in enumerate(halves(a_buf.at[z, y]) + [t_rx.at[1, other]]):
             pltpu.make_async_remote_copy(
                 src_ref=sent, dst_ref=sent,
                 send_sem=zsend.at[phase, other], recv_sem=zrecv.at[phase, other],
@@ -273,7 +278,7 @@
     own, rank = factor.shape[2:]
     nz, nx = nr // 2, ns // 2
     half = rows // 2
-    count = 2 * nz + 3 * (nx - 1) + 7
+    count = 3 * nz + 3 * (nx - 1) + 6
     slots = max(nx - 1, 1)
     scratch = [
         pltpu.VMEM((nz, 2, own, 2 * rank), BF16),
@@ -303,8 +308,8 @@
         pltpu.SemaphoreType.DMA((4,)),
         pltpu.SemaphoreType.DMA((count,)),
         pltpu.SemaphoreType.DMA((count,)),
-        pltpu.SemaphoreType.DMA((2, nz)),
-        pltpu.SemaphoreType.DMA((2, nz)),
+        pltpu.SemaphoreType.DMA((3, nz)),
+        pltpu.SemaphoreType.DMA((3, nz)),
         pltpu.SemaphoreType.REGULAR((nz,)),
         pltpu.SemaphoreType.REGULAR((nz,)),
     ]

time: 36.7 us -> 36.3 us (0.989)
  no operation moved by 1% of the time
where the time goes in v4:
time: 36.3 us; the launch traced here: 36.2 us
  Pallas kernels  34.7 us (96%)
  local copies, waits for them, and re-layouts  1.54 us (4%)
    pallas_call x1, Pallas kernels, body(): pl.pallas_call(functools.partial(kernel, nz, nx, scaling), out_shape=jax....  34.7 us
    unnamed x1, local copies, waits for them, and re-layouts  1.54 us

profile of v4, /device:TPU:0, one launch (start us, length us, event | category | flops | bytes accessed | tf_op | source)
XLA Modules:
  0.0 36.2 jit_solution(15598667062773168041)
XLA Ops:
  0.0 34.7 %gradient.1 = f32[2,1,96,128]{3,2,1,0:T(8,128)} custom-call(bf16[2,384,768]{2,1,0:T(8,128)(2,1)} %k_hbm.1, bf16[2,384,768]{2,1,0:T(8,128)(2,1)} %d_hbm.1, bf16[2,1,96,128]{3,2,1,0:T(8,128)(2,1)} %q_hbm.1), custom_call_target="tpu_custom_call" | custom-call | tf_op jit(solution)/shard_map/gradient/pallas_call | solution.py:317
  34.7 1.5 %copy.5 = f32[2,1,96,128]{3,2,1,0:T(8,128)} copy(f32[2,1,96,128]{3,2,1,0:T(8,128)} %gradient.1) | data formatting | bytes 196608
